TPU v7x, 32 devices: a whole 2x2x4 slice. The times are simulated.
32 devices in a mesh: parts: 2 (over y), slab: 4 (over z), blk: 2 (over x), head: 2 (over core).
Axes of the slice: x: 2, y: 2, z: 4, core: 2. Of those that a mesh axis runs over, the one named last changes fastest.
Arguments:
- features: bfloat16 [4096, 512], P(('parts', 'slab', 'blk')), parts along dimension 0, may hold values from -16 to 16
- cotangent: bfloat16 [4096, 512], P(('parts', 'slab', 'blk')), parts along dimension 0, may hold values from -6 to 6
- w_query: bfloat16 [512, 512], P(None, 'head'), may hold values from -0.25 to 0.25
- w_key: bfloat16 [512, 512], P(None, 'head'), may hold values from -0.25 to 0.25
- w_value: bfloat16 [512, 512], P(None, 'head'), may hold values from -0.25 to 0.25
- w_out: bfloat16 [512, 512], P('head'), may hold values from -0.25 to 0.25
- adjacency: int32 [32, 3], P(('parts', 'slab', 'blk')), parts along dimension 0, may hold values from 0 to 1, as said below
- partner: int32 [3, 32], P(None, ('parts', 'slab', 'blk')), parts along dimension 1, may hold values from 0 to 15, as said below
- node_order: int32 [4096], P(('parts', 'slab', 'blk')), parts along dimension 0, may hold values from 0 to 255, as said below
Outputs:
- grad_input: bfloat16 [4096, 512], P(('parts', 'slab', 'blk'), 'head'), parts along dimension 0
There are 2 independent parts, one for each index of `parts`. A program takes and returns all parts, laid end to end along the dimension named above; an argument that names none is the same for every part. Nothing has to cross between parts.
Inputs may be any that keep to these rules, and one draw needn't show every extreme that they name: `adjacency`: column 1 (the block itself) is always 1. partner[m, g] is the block at the same position among its device's 2 blocks, on the device of the same blk index in another slab; partner[m, partner[m, g]] = g. Of the 3 * 2 (matching, block) pairs of one device, at most 2 have their partner in one slab, and on every device exactly 2 do for some slab. `node_order`: within each device's 2 * 128 positions, a permutation of the device's rows.
All inputs are finite; a program needn't handle non-finite values.
Results may differ from a plain program's by a relative error of at most 0.013.
The roundings to bfloat16 on the way count: a program that leaves them out, or rounds other values in their place, can miss the bound.
Values may be sent and summed in bfloat16 or wider, within the bound.
A program may use at most 64 MiB of HBM per device.

v0:
```python
import jax
import jax.numpy as jnp
from jax import lax
from jax.sharding import PartitionSpec as P

HEAD_DIM = 64


def padded_2(shard, sides, width):
    for axis, dim in sides:
        count, length = (lax.axis_size(axis), shard.shape[dim])
        up = [(i, (i + 1) % count) for i in range(count)]
        down = [(j, i) for i, j in up]
        last = lax.slice_in_dim(shard, length - width, length, axis=dim)
        first = lax.slice_in_dim(shard, 0, width, axis=dim)
        before = lax.ppermute(last, axis, up)
        after = lax.ppermute(first, axis, down)
        shard = jnp.concatenate([before, shard, after], axis=dim)
    return shard


def from_behind(value, axis, steps):
    count = lax.axis_size(axis)
    pairs = [(source, (source + steps) % count) for source in range(count)]
    return lax.ppermute(value, axis, pairs)


def attend(queries, grad_rows, key_rows, values, switch, score_scale):
    block_len = queries.shape[1]
    scores = (
        jnp.einsum("gqhd,gkhd->ghqk", queries, key_rows, preferred_element_type=jnp.float32)
        * score_scale
    )
    keys_on = jnp.repeat(switch, block_len, axis=1)
    scores = jnp.where(keys_on[:, None, None, :], scores, -jnp.inf)
    row_peak = jnp.max(scores, axis=-1, keepdims=True)
    row_total = jnp.log(jnp.sum(jnp.exp(scores - row_peak), axis=-1, keepdims=True)) + row_peak
    attention = jnp.exp(scores - row_total)
    attention_low = attention.astype(jnp.bfloat16)
    mixed_rows = jnp.einsum(
        "ghqk,gkhd->gqhd", attention_low, values, preferred_element_type=jnp.float32
    )
    row_dot = jnp.transpose(jnp.sum(grad_rows.astype(jnp.float32) * mixed_rows, axis=-1), (0, 2, 1))
    grad_attention = jnp.einsum(
        "gqhd,gkhd->ghqk", grad_rows, values, preferred_element_type=jnp.float32
    )
    grad_scores = (attention * (grad_attention - row_dot[..., None])).astype(jnp.bfloat16)
    grad_query = score_scale * jnp.einsum(
        "ghqk,gkhd->gqhd", grad_scores, key_rows, preferred_element_type=jnp.float32
    )
    grad_key = score_scale * jnp.einsum(
        "ghqk,gqhd->gkhd", grad_scores, queries, preferred_element_type=jnp.float32
    )
    grad_value = jnp.einsum(
        "ghqk,gqhd->gkhd", attention_low, grad_rows, preferred_element_type=jnp.float32
    )
    return (grad_query, grad_key, grad_value, row_total[..., 0], row_dot)


def to_slots(stacked, slot_block, block_count):
    blocked = stacked.reshape((stacked.shape[0], block_count, -1) + stacked.shape[2:])
    padded = jnp.concatenate([blocked, jnp.zeros_like(blocked[:, :1])], axis=1)
    return jnp.take(padded, slot_block, axis=1)


def body(features, cotangent, w_query, w_key, w_value, w_out, adjacency, partner, node_order):
    rows_dev = features.shape[0]
    block_count = adjacency.shape[0]
    block_len = rows_dev // block_count
    feat_width = w_query.shape[1]
    head_count = feat_width // HEAD_DIM
    score_scale = HEAD_DIM ** (-0.5)
    slab_count = lax.axis_size("slab")
    cycle_len = lax.axis_size("blk") * block_count
    capacity = max(1, (3 * block_count + slab_count - 2) // (slab_count - 1))
    slot_count = slab_count * capacity
    item_count = 3 * block_count
    inputs = jnp.take(features, node_order, axis=0)
    upstream = jnp.take(cotangent, node_order, axis=0)
    query_rows = jnp.dot(inputs, w_query, preferred_element_type=jnp.float32).astype(jnp.bfloat16)
    key_rows = jnp.dot(inputs, w_key, preferred_element_type=jnp.float32).astype(jnp.bfloat16)
    value_rows = jnp.dot(inputs, w_value, preferred_element_type=jnp.float32).astype(jnp.bfloat16)
    contract = (((1,), (1,)), ((), ()))
    grad_mix = lax.dot_general(
        upstream, w_out, contract, preferred_element_type=jnp.float32
    ).astype(jnp.bfloat16)
    pair_rows = jnp.stack([key_rows, value_rows])
    item_dest = (partner // cycle_len).reshape(-1)
    order_ids = jnp.arange(item_count, dtype=jnp.int32)
    earlier = order_ids[None, :] < order_ids[:, None]
    same_dest = item_dest[None, :] == item_dest[:, None]
    item_rank = jnp.sum((earlier & same_dest).astype(jnp.int32), axis=1)
    item_slot = item_dest * capacity + item_rank
    slot_ids = jnp.arange(slot_count, dtype=jnp.int32)
    slot_hit = (item_slot[None, :] == slot_ids[:, None]).astype(jnp.int32)
    slot_used = jnp.sum(slot_hit, axis=1)
    slot_item = jnp.sum(slot_hit * order_ids[None, :], axis=1) + (1 - slot_used) * item_count
    slot_block = jnp.where(slot_used > 0, slot_item % block_count, block_count)
    widened = padded_2(pair_rows, (("blk", 1),), block_len)
    widened = widened.reshape(2, block_count + 2, block_len, feat_width)
    near_rows = jnp.stack(
        [widened[:, offset : offset + block_count] for offset in range(3)], axis=2
    )
    sent_slots = to_slots(pair_rows, slot_block, block_count)
    arrived = lax.all_to_all(sent_slots, "slab", split_axis=1, concat_axis=1, tiled=True)
    far_rows = jnp.take(arrived, item_slot, axis=1)
    far_rows = far_rows.reshape(2, 3, block_count, block_len, feat_width)
    far_rows = jnp.transpose(far_rows, (0, 2, 1, 3, 4))
    gathered = jnp.concatenate([near_rows, far_rows], axis=2)
    gathered = gathered.reshape(2, block_count, 6 * block_len, head_count, HEAD_DIM)
    switch = jnp.concatenate([adjacency > 0, jnp.ones((block_count, 3), dtype=bool)], axis=1)
    query_blocks = query_rows.reshape(block_count, block_len, head_count, HEAD_DIM)
    grad_blocks = grad_mix.reshape(block_count, block_len, head_count, HEAD_DIM)

    def halves(source):
        return source.reshape((2, block_count // 2) + source.shape[1:])

    def visit_half(pieces):
        return attend(pieces[0], pieces[1], pieces[2], pieces[3], pieces[4], score_scale)

    results = lax.map(
        visit_half,
        (
            halves(query_blocks),
            halves(grad_blocks),
            halves(gathered[0]),
            halves(gathered[1]),
            halves(switch),
        ),
    )
    merged = [output.reshape((block_count,) + output.shape[2:]) for output in results]
    grad_query, grad_key, grad_value, row_total, row_dot = merged
    key_grads = jnp.stack([grad_key, grad_value]).reshape(2, block_count, -1, block_len, feat_width)
    extended = jnp.zeros((2, block_count + 2, block_len, feat_width), jnp.float32)
    for offset in range(3):
        extended = extended.at[:, offset : offset + block_count].add(key_grads[:, :, offset])
    from_right = from_behind(extended[:, :1].astype(jnp.bfloat16), "blk", -1).astype(jnp.float32)
    from_left = from_behind(extended[:, block_count + 1 :].astype(jnp.bfloat16), "blk", 1).astype(
        jnp.float32
    )
    own_grads = extended[:, 1 : block_count + 1]
    own_grads = own_grads.at[:, block_count - 1 :].add(from_right)
    own_grads = own_grads.at[:, :1].add(from_left)
    far_terms = jnp.transpose(key_grads[:, :, 3:], (0, 2, 1, 3, 4)).reshape(
        2, item_count, block_len, feat_width
    )
    padded = jnp.concatenate([far_terms, jnp.zeros_like(far_terms[:, :1])], axis=1)
    outgoing = jnp.take(padded, slot_item, axis=1)
    returned = lax.all_to_all(
        outgoing.astype(jnp.bfloat16), "slab", split_axis=1, concat_axis=1, tiled=True
    ).astype(outgoing.dtype)
    returned_terms = jnp.take(returned, item_slot, axis=1).reshape(
        2, 3, block_count, block_len, feat_width
    )
    own_grads = own_grads + jnp.sum(returned_terms, axis=1)
    grad_low = own_grads.reshape(2, rows_dev, feat_width).astype(jnp.bfloat16)
    query_low = grad_query.reshape(rows_dev, feat_width).astype(jnp.bfloat16)
    partial_sum = lax.dot_general(query_low, w_query, contract, preferred_element_type=jnp.float32)
    partial_sum = partial_sum + lax.dot_general(
        grad_low[0], w_key, contract, preferred_element_type=jnp.float32
    )
    partial_sum = partial_sum + lax.dot_general(
        grad_low[1], w_value, contract, preferred_element_type=jnp.float32
    )
    placed = jnp.zeros_like(partial_sum).at[node_order].set(partial_sum)
    head_share = lax.psum_scatter(
        placed.astype(jnp.bfloat16), "head", scatter_dimension=1, tiled=True
    )
    return head_share


def solution(mesh):
    in_specs = (
        P(("parts", "slab", "blk"), None),
        P(("parts", "slab", "blk"), None),
        P(None, "head"),
        P(None, "head"),
        P(None, "head"),
        P("head", None),
        P(("parts", "slab", "blk"), None),
        P(None, ("parts", "slab", "blk")),
        P(("parts", "slab", "blk")),
    )
    out_specs = P(("parts", "slab", "blk"), "head")
    return jax.shard_map(body, mesh=mesh, in_specs=in_specs, out_specs=out_specs, check_vma=False)
```

profile of v0, /device:TPU:0, one launch (start us, length us, event | category | flops | bytes accessed | tf_op | source)
XLA Modules:
  0.0 128.6 jit_solution(15643832790657309337)
XLA Ops:
  6.5 0.7 compare_select_fusion.1
  7.3 0.7 compare_and_fusion
  8.0 0.8 copy.68
  9.2 0.5 compare_and_fusion.1
  9.7 2.2 %gather_fusion.4 = bf16[256,512]{1,0:T(8,128)(2,1)S(1)} fusion(bf16[256,512]{1,0:T(8,128)(2,1)} %param.23, s32[1024]{0:T(1024)S(1)} %pad_clamp_fusion.3), kind=kCustom, calls=%fused_computation.clone | custom fusion | bytes 525312 | tf_op jit(solution)/shard_map/jit(_take)/gather | solution.py:78
  12.0 0.3 convolution_convert_fusion.3
  12.3 0.3 convolution_convert_fusion.2
  12.6 0.6 gather_fusion
  13.2 1.1 select_bitcast_fusion
  14.3 6.5 %all-to-all-start = ((bf16[2,8,128,256]{3,2,0,1:T(8,128)(2,1)}), bf16[2,8,128,256]{3,2,0,1:T(8,128)(2,1)S(1)}, u32[]{:S(2)}, u32[]{:S(2)}) async-start(bf16[2,8,128,256]{3,2,0,1:T(8,128)(2,1)} %select_bitcast_fusion), calls=%async_computation | async-start | bytes 2097152 | tf_op jit(solution)/shard_map/all_to_all | solution.py:105
  20.8 1.6 %collective-permute-start = (bf16[2,128,256]{2,1,0:T(8,128)(2,1)S(1)}, bf16[2,128,256]{2,1,0:T(8,128)(2,1)S(1)}, u32[]{:S(2)}, u32[]{:S(2)}) collective-permute-start(bf16[2,128,256]{2,1,0:T(8,128)(2,1)S(1)} %get-tuple-element.185), channel_id=1, source_target_pairs={{0,2},{2,0},{1,3},{3,1},{4,6},{6,4},{5,7},{7,5},{8,10},{10,8},{9,1... | collective-permute-start | bytes 393224 | tf_op jit(solution)/shard_map/ppermute | solution.py:16
  22.4 0.5 collective-permute-start.1
  23.1 1.2 gather_fusion.5
  24.3 0.3 convolution_convert_fusion.1
  24.6 1.2 convolution_convert_fusion
  26.5 0.7 collective-permute-done
  27.2 1.4 %collective-permute-done.1 = bf16[2,128,256]{2,1,0:T(8,128)(2,1)S(1)} collective-permute-done((bf16[2,128,256]{2,1,0:T(8,128)(2,1)S(1)}, bf16[2,128,256]{2,1,0:T(8,128)(2,1)S(1)}, u32[]{:S(2)}, u32[]{:S(2)}) %collective-permute-start.1) | collective-permute-done | bytes 131104 | tf_op jit(solution)/shard_map/ppermute | solution.py:17
  28.8 17.8 %all-to-all-done = bf16[2,8,128,256]{3,2,0,1:T(8,128)(2,1)S(1)} async-done(((bf16[2,8,128,256]{3,2,0,1:T(8,128)(2,1)}), bf16[2,8,128,256]{3,2,0,1:T(8,128)(2,1)S(1)}, u32[]{:S(2)}, u32[]{:S(2)}) %all-to-all-start) | async-done | bytes 1048608 | tf_op jit(solution)/shard_map/all_to_all | solution.py:105
  46.5 0.6 gather_fusion.1
  47.6 0.8 copy.75
  48.4 0.9 reshape_squeeze.6
  49.3 0.8 copy.78
  50.1 0.9 reshape_squeeze.7
  51.0 10.3 %while.19 = (s32[]{:T(128)}, bf16[2,1,128,4,64]{2,4,3,1,0:T(8,128)(2,1)S(1)}, f32[2,1,768,4,64]{2,4,3,1,0:T(8,128)}, f32[2,1,768,4,64]{2,4,3,1,0:T(8,128)}, bf16...) while((s32[]{:T(128)}, ...), condition=%wide.region_7.9_spmd, body=%wide.region_3.0_spmd.sunk | while | flops 307428352 | bytes 26441652 | solution.py:121
  51.1 0.5 fusion.102
  51.6 0.4 exponential_reduce_fusion.2
  52.0 0.5 copy-done.2
  52.5 0.5 fusion.106
  52.9 0.6 fusion.103
  53.5 0.6 copy-done.3
  54.1 0.5 multiply_convert_fusion.2
  54.6 1.2 fusion.105
  55.7 0.4 fusion.104
  56.2 0.5 fusion.102
  56.7 0.4 exponential_reduce_fusion.2
  57.1 0.5 copy-done.2
  57.6 0.5 fusion.106
  58.1 0.6 fusion.103
  58.7 0.6 copy-done.3
  59.2 0.5 multiply_convert_fusion.2
  59.7 1.2 fusion.105
  60.9 0.4 fusion.104
  61.3 0.6 copy-done.9
  61.9 2.7 %stack.40 = f32[1,2,6,128,256]{3,2,4,1,0:T(8,128)} reshape(f32[2,1,768,4,64]{2,4,3,1,0:T(8,128)} %get-tuple-element.116) | data formatting | bytes 3145728 | tf_op jit(solution)/shard_map/stack | solution.py:133
  64.6 1.9 %copy.85 = f32[1,2,6,128,256]{4,3,1,0,2:T(8,128)S(1)} copy(f32[1,2,6,128,256]{3,2,4,1,0:T(8,128)} %stack.40) | data formatting | bytes 3145728 | tf_op jit(solution)/shard_map/stack | solution.py:133
  66.6 1.6 %stack.41 = f32[1,2,6,128,256]{3,2,4,1,0:T(8,128)} reshape(f32[2,1,768,4,64]{2,4,3,1,0:T(8,128)S(1)} %copy-done.4) | data formatting | bytes 3145728 | tf_op jit(solution)/shard_map/stack | solution.py:133
  68.2 1.8 %copy.86 = f32[1,2,6,128,256]{4,3,1,0,2:T(8,128)S(1)} copy(f32[1,2,6,128,256]{3,2,4,1,0:T(8,128)} %stack.41) | data formatting | bytes 3145728 | tf_op jit(solution)/shard_map/stack | solution.py:133
  70.2 1.1 concatenate.31
  71.3 2.8 %gather_fusion.2 = bf16[8,2,128,256]{3,2,1,0:T(8,128)(2,1)} fusion(bf16[2,7,128,256]{3,2,1,0:T(8,128)(2,1)} %concatenate.31, s32[1024]{0:T(1024)S(1)} %get-tuple-element.191), kind=kCustom, calls=%fused_computation.4 | custom fusion | bytes 2097184 | tf_op jit(solution)/shard_map/jit(_take)/gather | solution.py:148
  74.1 2.6 %fusion.34 = bf16[2,8,128,256]{3,2,0,1:T(8,128)(2,1)} fusion(bf16[8,2,128,256]{3,2,1,0:T(8,128)(2,1)} %gather_fusion.2, pred[8]{0:T(512)(128)(4,1)S(1)} %copy-done.11), kind=kLoop, calls=%fused_computation.60 | loop fusion | flops 524288 | bytes 2097160 | tf_op jit(solution)/shard_map/convert_element_type | solution.py:150
  76.7 4.3 %all-to-all-start.1 = ((bf16[2,8,128,256]{3,2,0,1:T(8,128)(2,1)}), bf16[2,8,128,256]{3,2,0,1:T(8,128)(2,1)}, u32[]{:S(2)}, u32[]{:S(2)}) async-start(bf16[2,8,128,256]{3,2,0,1:T(8,128)(2,1)} %fusion.34), calls=%async_computation.1 | async-start | bytes 2097152 | tf_op jit(solution)/shard_map/all_to_all | solution.py:149
  81.6 1.6 %collective-permute-start.2 = (bf16[2,1,128,256]{3,2,1,0:T(8,128)(2,1)S(1)}, bf16[2,1,128,256]{3,2,1,0:T(8,128)(2,1)S(1)}, u32[]{:S(2)}, u32[]{:S(2)}) collective-permute-start(bf16[2,1,128,256]{3,2,1,0:T(8,128)(2,1)S(1)} %slice.266), channel_id=1, source_target_pairs={{0,2},{2,0},{1,3},{3,1},{4,6},{6,4},{5,7},{7,5},{8,10},{10,8},{9,1... | collective-permute-start | bytes 393224 | tf_op jit(solution)/shard_map/ppermute | solution.py:25
  83.2 0.5 collective-permute-start.3
  83.9 0.3 fusion.48
  84.1 3.4 %collective-permute-done.2 = bf16[2,1,128,256]{3,2,1,0:T(8,128)(2,1)S(1)} collective-permute-done((bf16[2,1,128,256]{3,2,1,0:T(8,128)(2,1)S(1)}, bf16[2,1,128,256]{3,2,1,0:T(8,128)(2,1)S(1)}, u32[]{:S(2)}, u32[]{:S(2)}) %collective-permute-start.2) | collective-permute-done | bytes 131104 | tf_op jit(solution)/shard_map/ppermute | solution.py:25
  87.6 1.4 %collective-permute-done.3 = bf16[2,1,128,256]{3,2,1,0:T(8,128)(2,1)S(1)} collective-permute-done((bf16[2,1,128,256]{3,2,1,0:T(8,128)(2,1)S(1)}, bf16[2,1,128,256]{3,2,1,0:T(8,128)(2,1)S(1)}, u32[]{:S(2)}, u32[]{:S(2)}) %collective-permute-start.3) | collective-permute-done | bytes 131104 | tf_op jit(solution)/shard_map/ppermute | solution.py:25
  89.0 17.2 %all-to-all-done.1 = bf16[2,8,128,256]{3,2,0,1:T(8,128)(2,1)} async-done(((bf16[2,8,128,256]{3,2,0,1:T(8,128)(2,1)}), bf16[2,8,128,256]{3,2,0,1:T(8,128)(2,1)}, u32[]{:S(2)}, u32[]{:S(2)}) %all-to-all-start.1) | async-done | bytes 1048608 | tf_op jit(solution)/shard_map/all_to_all | solution.py:149
  106.2 1.4 %convert_element_type.78 = f32[2,8,128,256]{3,2,0,1:T(8,128)S(1)} convert(bf16[2,8,128,256]{3,2,0,1:T(8,128)(2,1)} %all-to-all-done.1) | non-fusion elementwise | flops 524288 | bytes 3145728 | tf_op jit(solution)/shard_map/convert_element_type | solution.py:151
  107.7 1.8 %gather_fusion.3 = f32[6,2,128,256]{3,2,1,0:T(8,128)} fusion(f32[2,8,128,256]{3,2,0,1:T(8,128)S(1)} %convert_element_type.78, s32[1024]{0:T(1024)S(1)} %pad_clamp_fusion.1), kind=kCustom, calls=%fused_computation.5 | custom fusion | bytes 3145752 | tf_op jit(solution)/shard_map/jit(_take)/gather | solution.py:152
  109.4 1.6 %copy.88 = f32[2,6,128,256]{3,2,1,0:T(8,128)S(1)} copy(f32[2,6,128,256]{3,2,0,1:T(8,128)} %bitcast.204) | data formatting | bytes 3145728 | tf_op jit(solution)/shard_map/jit(_take)/gather | solution.py:152
  111.4 0.6 copy-done.6
  112.5 1.6 %scatter_custom_fusion = f32[256,512]{1,0:T(8,128)S(1)} fusion(s32[256]{0:T(256)S(1)} %compare_select_fusion.1, f32[256,512]{1,0:T(8,128)S(1)} %convolution_add_fusion, f32[]{:T(128)} %constant.251.clone.1), kind=kCustom, calls=%fused_computation.87 | custom fusion | bytes 524292 | tf_op jit(solution)/shard_map/scatter | solution.py:165
  114.1 0.7 convert_element_type.80
  114.9 6.9 %reduce-scatter.2.cloned.1.call-done = bf16[256,256]{1,0:T(8,128)(2,1)} async-done(((bf16[256,512]{1,0:T(8,128)(2,1)}), bf16[256,256]{1,0:T(8,128)(2,1)}) %reduce-scatter.2.cloned.1.call-update) | async-done | bytes 131088 | tf_op jit(solution)/shard_map/reduce_scatter | solution.py:166
  (80 shorter events, 4.0 us)
Async XLA Ops:
  6.5 17.8 %copy-start = (bf16[512,256]{1,0:T(8,128)(2,1)S(1)}, bf16[512,256]{1,0:T(8,128)(2,1)}, u32[]{:S(2)}) copy-start(bf16[512,256]{1,0:T(8,128)(2,1)} %param.25) | copy-start | bytes 786436
  6.5 5.4 %copy-start.5 = (bf16[512,256]{1,0:T(8,128)(2,1)S(1)}, bf16[512,256]{1,0:T(8,128)(2,1)}, u32[]{:S(2)}) copy-start(bf16[512,256]{1,0:T(8,128)(2,1)} %param.26) | copy-start | bytes 786436
  9.7 2.5 %copy-start.7 = (bf16[512,256]{1,0:T(8,128)(2,1)S(1)}, bf16[512,256]{1,0:T(8,128)(2,1)}, u32[]{:S(2)}) copy-start(bf16[512,256]{1,0:T(8,128)(2,1)} %param.27) | copy-start | bytes 786436
  14.3 8.7 %copy-start.1 = (bf16[256,512]{1,0:T(8,128)(2,1)S(1)}, bf16[256,512]{1,0:T(8,128)(2,1)}, u32[]{:S(2)}) copy-start(bf16[256,512]{1,0:T(8,128)(2,1)} %param.24) | copy-start | bytes 786436
  14.3 32.2 %all-to-all-start = ((bf16[2,8,128,256]{3,2,0,1:T(8,128)(2,1)}), bf16[2,8,128,256]{3,2,0,1:T(8,128)(2,1)S(1)}, u32[]{:S(2)}, u32[]{:S(2)}) async-start(bf16[2,8,128,256]{3,2,0,1:T(8,128)(2,1)} %select_bitcast_fusion), calls=%async_computation | async-start | bytes 2097152 | tf_op jit(solution)/shard_map/all_to_all | solution.py:105
  20.8 3.4 %copy-start.12 = (s32[2,3]{1,0:T(2,128)S(1)}, s32[2,3]{1,0:T(2,128)}, u32[]{:S(2)}) copy-start(s32[2,3]{1,0:T(2,128)} %param.29) | copy-start | bytes 76
  20.8 6.4 %collective-permute-start = (bf16[2,128,256]{2,1,0:T(8,128)(2,1)S(1)}, bf16[2,128,256]{2,1,0:T(8,128)(2,1)S(1)}, u32[]{:S(2)}, u32[]{:S(2)}) collective-permute-start(bf16[2,128,256]{2,1,0:T(8,128)(2,1)S(1)} %get-tuple-element.185), channel_id=1, source_target_pairs={{0,2},{2,0},{1,3},{3,1},{4,6},{6,4},{5,7},{7,5},{8,10},{10,8},{9,1... | collective-permute-start | bytes 393224 | tf_op jit(solution)/shard_map/ppermute | solution.py:16
  22.4 6.3 %collective-permute-start.1 = (bf16[2,128,256]{2,1,0:T(8,128)(2,1)S(1)}, bf16[2,128,256]{2,1,0:T(8,128)(2,1)S(1)}, u32[]{:S(2)}, u32[]{:S(2)}) collective-permute-start(bf16[2,128,256]{2,1,0:T(8,128)(2,1)S(1)} %get-tuple-element.186), channel_id=1, source_target_pairs={{2,0},{0,2},{3,1},{1,3},{6,4},{4,6},{7,5},{5,7},{10,8},{8,10},{11,... | collective-permute-start | bytes 393224 | tf_op jit(solution)/shard_map/ppermute | solution.py:17
  51.1 1.4 %copy-start.2 = (f32[2,1,768,4,64]{2,4,3,1,0:T(8,128)S(1)}, f32[2,1,768,4,64]{2,4,3,1,0:T(8,128)}, u32[]{:S(2)}) copy-start(f32[2,1,768,4,64]{2,4,3,1,0:T(8,128)} %get-tuple-element.265) | copy-start | bytes 4718596 | tf_op jit(solution)/shard_map/while
  52.9 1.1 copy-start.3
  56.2 1.4 %copy-start.2 = (f32[2,1,768,4,64]{2,4,3,1,0:T(8,128)S(1)}, f32[2,1,768,4,64]{2,4,3,1,0:T(8,128)}, u32[]{:S(2)}) copy-start(f32[2,1,768,4,64]{2,4,3,1,0:T(8,128)} %get-tuple-element.265) | copy-start | bytes 4718596 | tf_op jit(solution)/shard_map/while
  58.1 1.1 copy-start.3
  61.3 0.7 copy-start.9
  64.6 2.0 %copy-start.4 = (f32[2,1,768,4,64]{2,4,3,1,0:T(8,128)S(1)}, f32[2,1,768,4,64]{2,4,3,1,0:T(8,128)}, u32[]{:S(2)}) copy-start(f32[2,1,768,4,64]{2,4,3,1,0:T(8,128)} %get-tuple-element.117) | copy-start | bytes 4718596
  70.2 3.8 %copy-start.11 = (pred[8]{0:T(512)(128)(4,1)S(1)}, pred[8]{0:T(512)(128)(4,1)}, u32[]{:S(2)}) copy-start(pred[8]{0:T(512)(128)(4,1)} %get-tuple-element.187) | copy-start | bytes 28
  76.7 29.5 %all-to-all-start.1 = ((bf16[2,8,128,256]{3,2,0,1:T(8,128)(2,1)}), bf16[2,8,128,256]{3,2,0,1:T(8,128)(2,1)}, u32[]{:S(2)}, u32[]{:S(2)}) async-start(bf16[2,8,128,256]{3,2,0,1:T(8,128)(2,1)} %fusion.34), calls=%async_computation.1 | async-start | bytes 2097152 | tf_op jit(solution)/shard_map/all_to_all | solution.py:149
  80.9 40.9 %reduce-scatter.2.cloned.1.call-start = ((), (), s32[]{:S(2)}) async-start(), calls=%async_computation.3 | async-start | bytes 393216 | tf_op jit(solution)/shard_map/reduce_scatter | solution.py:166
  81.5 2.2 %copy-start.10 = (bf16[2,1,128,4,64]{2,4,3,1,0:T(8,128)(2,1)S(1)}, bf16[2,1,128,4,64]{2,4,3,1,0:T(8,128)(2,1)}, u32[]{:S(2)}) copy-start(bf16[2,1,128,4,64]{2,4,3,1,0:T(8,128)(2,1)} %copy-done.9) | copy-start | bytes 393220
  81.6 5.9 %collective-permute-start.2 = (bf16[2,1,128,256]{3,2,1,0:T(8,128)(2,1)S(1)}, bf16[2,1,128,256]{3,2,1,0:T(8,128)(2,1)S(1)}, u32[]{:S(2)}, u32[]{:S(2)}) collective-permute-start(bf16[2,1,128,256]{3,2,1,0:T(8,128)(2,1)S(1)} %slice.266), channel_id=1, source_target_pairs={{0,2},{2,0},{1,3},{3,1},{4,6},{6,4},{5,7},{7,5},{8,10},{10,8},{9,1... | collective-permute-start | bytes 393224 | tf_op jit(solution)/shard_map/ppermute | solution.py:25
  83.2 5.8 %collective-permute-start.3 = (bf16[2,1,128,256]{3,2,1,0:T(8,128)(2,1)S(1)}, bf16[2,1,128,256]{3,2,1,0:T(8,128)(2,1)S(1)}, u32[]{:S(2)}, u32[]{:S(2)}) collective-permute-start(bf16[2,1,128,256]{3,2,1,0:T(8,128)(2,1)S(1)} %slice.265), channel_id=1, source_target_pairs={{0,2},{2,0},{1,3},{3,1},{4,6},{6,4},{5,7},{7,5},{8,10},{10,8},{9,1... | collective-permute-start | bytes 393224 | tf_op jit(solution)/shard_map/ppermute | solution.py:25
  111.0 1.0 copy-start.6
  111.2 1.0 copy-start.8
Sparse Core Ops, SparseCore 0:
  115.0 6.7 reduce-scatter.1
where the time goes:
time: 129 us
  waiting for transfers between devices  48.8 us (38%)
  local copies, waits for them, and re-layouts  30.6 us (24%)
  starting transfers between devices  15.1 us (12%)
  between operations  13.9 us (11%)
  other arithmetic  10.2 us (8%)
  matrix products  9.91 us (8%)
    all_to_all x1, waiting for transfers between devices, body(): lax.all_to_all(sent_slots, 'slab', split_axis=1, concat_axis=1, tiled=True)  17.8 us
    all_to_all x1, waiting for transfers between devices, body(): lax.all_to_all(outgoing.astype(jnp.bfloat16), 'slab', split_axis=1, conca...  17.2 us
    another operation x4, local copies, waits for them, and re-layouts, body(): jnp.stack([grad_key, grad_value])  8.01 us
    reduce_scatter x1, waiting for transfers between devices, body(): lax.psum_scatter(placed.astype(jnp.bfloat16), 'head', scatter_dimension=1...  6.94 us
    all_to_all x1, starting transfers between devices, body(): lax.all_to_all(sent_slots, 'slab', split_axis=1, concat_axis=1, tiled=True)  6.45 us
    ppermute x2, waiting for transfers between devices, from_behind(): return lax.ppermute(value, axis, pairs)  4.81 us
    all_to_all x1, starting transfers between devices, body(): lax.all_to_all(outgoing.astype(jnp.bfloat16), 'slab', split_axis=1, conca...  4.25 us
    gather x2, local copies, waits for them, and re-layouts, body(): jnp.take(returned, item_slot, axis=1)  3.38 us
  transfers between devices with their start and end apart: 7, of which 7 were waited for; matrix products, arithmetic and copies ran while one was open for 4% of the time, Pallas kernels for 0%

commit v1 on v0

v1 whole, which is shorter than its diff:
```python
import functools

import jax
import jax.numpy as jnp
from jax import lax
from jax.experimental import pallas as pl
from jax.experimental.pallas import tpu as pltpu
from jax.sharding import PartitionSpec as P

HEAD_DIM = 64
OFF = -1e30
NT = (((1,), (1,)), ((), ()))
TN = (((0,), (0,)), ((), ()))
F32, BF16 = jnp.float32, jnp.bfloat16
MESH = pl.DeviceIdType.MESH


def mm(a, b):
    return jnp.dot(a, b, preferred_element_type=F32)


def mm_nt(a, b):
    return lax.dot_general(a, b, NT, preferred_element_type=F32)


def kernel(
    n, nb,
    feat, cot, w_q, w_k, w_v, w_o, adj, part, order, out,
    perm, own_x, own_c, rx, rc, k_own, v_own, kt_own, qm_own, gm_own,
    kt_far, qm_far, s_loc, g_loc, s_far, g_far, s_back, peak, stat, stat_far,
    dq, dk, dv, give, take,
    x_send, x_recv, xf_send, xf_recv, c_send, c_recv, cf_send, cf_recv,
    t_send, t_recv, h_send, h_recv,
):
    rows, width = feat.shape
    half = width // 2
    cols = w_q.shape[1]
    heads = cols // HEAD_DIM
    block = rows // 2
    scale = HEAD_DIM ** -0.5
    h, slab, x = (lax.axis_index(a) for a in ("head", "slab", "blk"))
    behind, ahead = {"blk": lax.rem(x + nb - 1, nb)}, {"blk": lax.rem(x + 1, nb)}
    twin = {"head": 1 - h}

    def onward(d):
        return {"slab": lax.rem(slab + d, n)}

    def each(f):
        if n <= 4:
            for d in sorted(range(1, n), key=lambda d: (min(d, n - d), d)):
                f(d)
        else:
            lax.fori_loop(1, n, lambda d, c: (f(d), c)[1], 0)

    barrier = pltpu.get_barrier_semaphore()

    def greet(where):
        pl.semaphore_signal(barrier, inc=1, device_id=where, device_id_type=MESH)

    greet(behind)
    greet(ahead)
    greet(twin)
    each(lambda d: greet(onward(d)))

    def copy(src, dst, send, recv, where):
        return pltpu.make_async_remote_copy(
            src_ref=src, dst_ref=dst, send_sem=send, recv_sem=recv,
            device_id=where, device_id_type=MESH,
        )

    low, high = pl.ds(0, block), pl.ds(block, block)

    def near_copies(own, far, send, recv):
        return (
            copy(own.at[h, low], far.at[0, h, high], send.at[n], recv.at[n], behind),
            copy(own.at[h, high], far.at[0, h, low], send.at[0], recv.at[0], ahead),
        )

    def slab_copy(own, far, send, recv, d):
        return copy(own.at[h], far.at[d, h], send.at[d], recv.at[d], onward(d))

    def twin_copy(far, send, recv, i):
        return copy(far.at[i, h], far.at[i, h], send.at[i], recv.at[i], twin)

    x_near = functools.partial(near_copies, own_x, rx, x_send, x_recv)
    c_near = functools.partial(near_copies, own_c, rc, c_send, c_recv)
    x_slab = functools.partial(slab_copy, own_x, rx, x_send, x_recv)
    c_slab = functools.partial(slab_copy, own_c, rc, c_send, c_recv)
    x_twin = functools.partial(twin_copy, rx, xf_send, xf_recv)
    c_twin = functools.partial(twin_copy, rc, cf_send, cf_recv)

    def stat_near():
        return (
            copy(stat.at[0], stat_far.at[0, 1], t_send.at[n], t_recv.at[n], behind),
            copy(stat.at[1], stat_far.at[0, 0], t_send.at[0], t_recv.at[0], ahead),
        )

    def stat_slab(d):
        return copy(stat, stat_far.at[d], t_send.at[d], t_recv.at[d], onward(d))

    hot = lax.broadcasted_iota(jnp.int32, (rows, rows), 0) == order[...]
    perm[...] = jnp.where(hot, 1.0, 0.0).astype(BF16)
    x_all = lax.dot_general(perm[...], feat[...], TN, preferred_element_type=F32).astype(BF16)
    own_x[0] = x_all[:, :half]
    own_x[1] = x_all[:, half:]
    pl.semaphore_wait(barrier, n + 2)
    for c in x_near():
        c.start()
    each(lambda d: x_slab(d).start())

    c_all = lax.dot_general(perm[...], cot[...], TN, preferred_element_type=F32).astype(BF16)
    own_c[0] = c_all[:, :half]
    own_c[1] = c_all[:, half:]

    lane_head = lax.broadcasted_iota(jnp.int32, (1, cols), 1) // HEAD_DIM
    masks = [jnp.where(lane_head == i, 1.0, 0.0).astype(BF16) for i in range(heads)]

    def masked(value, b):
        part_rows = value[b * block:(b + 1) * block]
        return jnp.concatenate([part_rows * mask for mask in masks], axis=0)

    def weight_flag(flag):
        return jnp.where(flag > 0, 1.0, 0.0).astype(F32)

    def far_weight(i, b):
        if isinstance(i, int) and i == 0:
            return weight_flag(adj[0, 0] if b == 0 else adj[1, 2])
        source = lax.rem(slab + n - i, n)
        total = jnp.float32(0.0)
        for m in range(3):
            total = total + jnp.where(lax.div(part[m, b], 2 * nb) == source, 1.0, 0.0)
        return total

    def local_weight(kb, qb):
        if kb == qb:
            return jnp.float32(1.0)
        return weight_flag(adj[0, 2] if qb == 0 else adj[1, 0])

    def bias(w):
        return jnp.where(w > 0.0, 0.0, OFF).astype(F32)

    q_all = (mm(x_all, w_q[...]).astype(BF16) * scale).astype(BF16)
    k_all = mm(x_all, w_k[...])
    k_own[...] = k_all.astype(BF16)
    kt_own[...] = k_all.T.astype(BF16)
    v_own[...] = mm(x_all, w_v[...]).astype(BF16)
    g_all = mm_nt(c_all, w_o[...]).astype(BF16)
    for b in range(2):
        qm_own[b] = masked(q_all, b)
        gm_own[b] = masked(g_all, b)
    for c in c_near():
        c.start()
    each(lambda d: c_slab(d).start())
    for b in range(2):
        s = mm_nt(k_own[...], qm_own[b])
        s_loc[b] = s
        g_loc[b] = mm_nt(v_own[...], gm_own[b])
        top = [
            jnp.max(s[kb * block:(kb + 1) * block], axis=0, keepdims=True)
            + bias(local_weight(kb, b))
            for kb in range(2)
        ]
        peak[b] = jnp.maximum(top[0], top[1])

    def forward_slot(i):
        x0, x1 = rx[i, 0], rx[i, 1]

        def project(w):
            return mm(x0, w[:half, :]) + mm(x1, w[half:, :])

        q = (project(w_q).astype(BF16) * scale).astype(BF16)
        k32 = project(w_k)
        k = k32.astype(BF16)
        kt_far[i] = k32.T.astype(BF16)
        v = project(w_v).astype(BF16)
        for b in range(2):
            here = slice(b * block, (b + 1) * block)
            qm = masked(q, b)
            qm_far[i, b] = qm
            s = mm_nt(k[here], qm_own[b])
            s_far[i, b] = s
            g_far[i, b] = mm_nt(v[here], gm_own[b])
            s_back[i, b] = mm_nt(k_own[here, :], qm)
            top = jnp.max(s, axis=0, keepdims=True) + bias(far_weight(i, b))
            peak[b] = jnp.maximum(peak[b], top)

    for c in x_near():
        c.wait_recv()
    x_twin(0).start()
    x_twin(0).wait_recv()
    forward_slot(0)

    def take_x(d):
        x_slab(d).wait_recv()
        x_twin(d).start()
        x_twin(d).wait_recv()
        forward_slot(d)

    each(take_x)

    for b in range(2):
        qcols = slice(b * block, (b + 1) * block)
        top = peak[b]

        def expo(ref, at, w, total):
            e = jnp.exp(ref[at] + (bias(w) - top))
            ref[at] = e
            return total + w * jnp.sum(e, axis=0, keepdims=True)

        def loc(kb):
            return (b, slice(kb * block, (kb + 1) * block))

        total = jnp.zeros((1, heads * block), F32)
        for kb in range(2):
            total = expo(s_loc, loc(kb), local_weight(kb, b), total)
        total = expo(s_far, (0, b), far_weight(0, b), total)
        stat[b, 0:1] = total

        def far_expo(d):
            stat[b, 0:1] = expo(s_far, (d, b), far_weight(d, b), stat[b, 0:1])

        each(far_expo)
        total = stat[b, 0:1]
        inverse = 1.0 / total

        def weigh(sref, gref, at, w):
            p = sref[at] * (w * inverse)
            sref[at] = p
            low_p = p.astype(BF16).astype(F32)
            return jnp.sum(low_p * gref[at], axis=0, keepdims=True)

        dot = weigh(s_far, g_far, (0, b), far_weight(0, b))
        for kb in range(2):
            dot = dot + weigh(s_loc, g_loc, loc(kb), local_weight(kb, b))
        stat[b, 1:2] = dot

        def far_weigh(d):
            stat[b, 1:2] = stat[b, 1:2] + weigh(s_far, g_far, (d, b), far_weight(d, b))

        each(far_weigh)
        stat[b, 0:1] = top + jnp.log(total)
        flag = weight_flag(adj[0, 0] if b == 0 else adj[1, 2])
        stat[b, 2:3] = jnp.zeros((1, heads * block), F32) + flag
        stat[b, 3:8] = jnp.zeros((5, heads * block), F32)
    for c in stat_near():
        c.start()
    each(lambda d: stat_slab(d).start())

    for b in range(2):
        qcols = slice(b * block, (b + 1) * block)
        dot = stat[b, 1:2]
        p = s_loc[b]
        ds = (p * (g_loc[b] - dot)).astype(BF16)
        p_low = p.astype(BF16)
        if b == 0:
            dv[...] = mm(p_low, gm_own[b])
            dk[...] = mm(ds, qm_own[b])
        else:
            dv[...] += mm(p_low, gm_own[b])
            dk[...] += mm(ds, qm_own[b])
        for i in range(heads):
            hd = slice(i * HEAD_DIM, (i + 1) * HEAD_DIM)
            dq[hd, qcols] = mm(kt_own[hd, :], ds[:, i * block:(i + 1) * block])

        def query_grad(i):
            ds_i = (s_far[i, b] * (g_far[i, b] - stat[b, 1:2])).astype(BF16)
            for j in range(heads):
                hd = slice(j * HEAD_DIM, (j + 1) * HEAD_DIM)
                dq[hd, qcols] += mm(kt_far[i, hd, qcols], ds_i[:, j * block:(j + 1) * block])

        query_grad(0)
        each(query_grad)

    def backward_slot(i):
        c0, c1 = rc[i, 0], rc[i, 1]
        g = (mm_nt(c0, w_o[:, :half]) + mm_nt(c1, w_o[:, half:])).astype(BF16)
        for b in range(2):
            here = slice(b * block, (b + 1) * block)
            gm = masked(g, b)
            row_total = stat_far[i, b, 0:1]
            dot = stat_far[i, b, 1:2]
            if isinstance(i, int) and i == 0:
                w = stat_far[i, b, 2:3]
            else:
                w = jnp.zeros((1, heads * block), F32) + far_weight(i, b)
            p = jnp.exp(s_back[i, b] - jnp.where(w > 0.0, row_total, -OFF)) * w
            gp = mm_nt(v_own[here, :], gm)
            ds = (p * (gp - dot)).astype(BF16)
            dv[here, :] += mm(p.astype(BF16), gm)
            dk[here, :] += mm(ds, qm_far[i, b])

    for c in c_near():
        c.wait_recv()
    c_twin(0).start()
    c_twin(0).wait_recv()
    for c in stat_near():
        c.wait_recv()
    backward_slot(0)

    def take_c(d):
        c_slab(d).wait_recv()
        c_twin(d).start()
        c_twin(d).wait_recv()
        stat_slab(d).wait_recv()
        backward_slot(d)

    each(take_c)

    dq_low = (dq[...].T * scale).astype(BF16)
    dk_low, dv_low = dk[...].astype(BF16), dv[...].astype(BF16)

    def share(which):
        at = pl.ds(pl.multiple_of(which * half, half), half)
        return mm_nt(dq_low, w_q[at, :]) + mm_nt(dk_low, w_k[at, :]) + mm_nt(dv_low, w_v[at, :])

    give[...] = share(1 - h).astype(BF16)
    swap = copy(give, take, h_send, h_recv, twin)
    swap.start()
    mine = share(h)
    swap.wait_recv()
    branch = (mine + take[...].astype(F32)).astype(BF16)
    out[...] = mm(perm[...], branch).astype(BF16)

    swap.wait_send()
    for c in (*x_near(), *c_near(), *stat_near(), x_twin(0), c_twin(0)):
        c.wait_send()

    def finish(d):
        for c in (x_slab(d), c_slab(d), stat_slab(d), x_twin(d), c_twin(d)):
            c.wait_send()

    each(finish)


def body(features, cotangent, w_query, w_key, w_value, w_out, adjacency, partner, node_order):
    n, nb = lax.axis_size("slab"), lax.axis_size("blk")
    rows, width = features.shape
    cols = w_query.shape[1]
    half, block = width // 2, rows // 2
    lanes = (cols // HEAD_DIM) * block
    vm, dma = pltpu.VMEM, pltpu.SemaphoreType.DMA
    vmem, smem = (pl.BlockSpec(memory_space=m) for m in (pltpu.VMEM, pltpu.SMEM))
    return pl.pallas_call(
        functools.partial(kernel, n, nb),
        out_shape=jax.ShapeDtypeStruct((rows, half), BF16),
        in_specs=[vmem] * 6 + [smem] * 2 + [vmem],
        out_specs=vmem,
        scratch_shapes=[
            vm((rows, rows), BF16),
            vm((2, rows, half), BF16), vm((2, rows, half), BF16),
            vm((n, 2, rows, half), BF16), vm((n, 2, rows, half), BF16),
            vm((rows, cols), BF16), vm((rows, cols), BF16), vm((cols, rows), BF16),
            vm((2, lanes, cols), BF16), vm((2, lanes, cols), BF16),
            vm((n, cols, rows), BF16), vm((n, 2, lanes, cols), BF16),
            vm((2, rows, lanes), F32), vm((2, rows, lanes), F32),
            vm((n, 2, block, lanes), F32), vm((n, 2, block, lanes), F32),
            vm((n, 2, block, lanes), F32),
            vm((2, 1, lanes), F32), vm((2, 8, lanes), F32), vm((n, 2, 8, lanes), F32),
            vm((cols, rows), F32), vm((rows, cols), F32), vm((rows, cols), F32),
            vm((rows, half), BF16), vm((rows, half), BF16),
        ] + [dma((n + 1,)), dma((n + 1,)), dma((n,)), dma((n,))] * 2
        + [dma((n + 1,)), dma((n + 1,)), dma(()), dma(())],
        compiler_params=pltpu.CompilerParams(
            collective_id=0, has_side_effects=True, vmem_limit_bytes=52 * 1024 * 1024
        ),
    )(
        features, cotangent, w_query, w_key, w_value, w_out,
        adjacency, partner, node_order.reshape(1, rows),
    )


def solution(mesh):
    rows = P(("parts", "slab", "blk"), None)
    in_specs = (
        rows, rows,
        P(None, "head"), P(None, "head"), P(None, "head"), P("head", None),
        rows, P(None, ("parts", "slab", "blk")), P(("parts", "slab", "blk")),
    )
    return jax.shard_map(
        body, mesh=mesh, in_specs=in_specs,
        out_specs=P(("parts", "slab", "blk"), "head"), check_vma=False,
    )
```

time: 129 us -> 45.9 us (0.36)
  waiting for transfers between devices: 48.8 us -> 0 us
  Pallas kernels: 0 us -> 37.8 us
  local copies, waits for them, and re-layouts: 30.6 us -> 7.73 us
  starting transfers between devices: 15.1 us -> 0 us
  between operations: 13.9 us -> 0.02 us
  other arithmetic: 10.2 us -> 0 us
  matrix products: 9.91 us -> 0 us
    pallas_call x0 -> x1, Pallas kernels: none -> 37.8 us  [body(): pl.pallas_call(functools.partial(kernel, n, nb), out_shape=jax.ShapeDtype...]
    all_to_all x2 -> x0, waiting for transfers between devices: 34.9 us -> none  [the longest x1 17.8 us: body(): lax.all_to_all(sent_slots, 'slab', split_axis=1, concat_axis=1, tiled=True)]
    gather x8 -> x0, local copies, waits for them, and re-layouts: 10.8 us -> none  [the longest x2 3.38 us: body(): jnp.take(returned, item_slot, axis=1)]
    all_to_all x2 -> x0, starting transfers between devices: 10.7 us -> none  [the longest x1 6.45 us: body(): lax.all_to_all(sent_slots, 'slab', split_axis=1, concat_axis=1, tiled=True)]
    another operation x9 -> x0, local copies, waits for them, and re-layouts: 10.2 us -> none  [the longest x4 8.01 us: body(): jnp.stack([grad_key, grad_value])]
    dot_general x19 -> x0, matrix products: 9.91 us -> none  [the longest x2 2.31 us: attend(): jnp.einsum('ghqk,gqhd->gkhd', grad_scores, queries, preferred_element_typ...]
    reduce_scatter x1 -> x0, waiting for transfers between devices: 6.94 us -> none  [body(): lax.psum_scatter(placed.astype(jnp.bfloat16), 'head', scatter_dimension=1...]
    ppermute x4 -> x0, waiting for transfers between devices: 6.94 us -> none  [the longest x2 4.81 us: from_behind(): return lax.ppermute(value, axis, pairs)]
  transfers between devices with their start and end apart: 7 -> 0, of which waited for: 7 -> 0; matrix products, arithmetic and copies ran while one was open for 4% -> 0% of each run, Pallas kernels for 0% -> 0%
where the time goes in v1:
time: 45.9 us; the launch traced here: 45.6 us
  Pallas kernels  37.8 us (82%)
  local copies, waits for them, and re-layouts  7.73 us (17%)
    pallas_call x1, Pallas kernels, body(): pl.pallas_call(functools.partial(kernel, n, nb), out_shape=jax.ShapeDtype...  37.8 us
    unnamed x20, local copies, waits for them, and re-layouts  7.73 us

profile of v1, /device:TPU:0, one launch (start us, length us, event | category | flops | bytes accessed | tf_op | source)
XLA Modules:
  0.0 45.6 jit_solution(15343977955944928539)
XLA Ops:
  0.0 0.0 copy-start.8
  0.0 0.7 %copy-done.8 = s32[3,2]{0,1:T(2,128)S(1)} copy-done((s32[3,2]{0,1:T(2,128)S(1)}, s32[3,2]{0,1:T(2,128)}, u32[]{:S(2)}) %copy-start.8) | copy-done | bytes 48
  0.7 0.0 copy-start.6
  0.7 0.0 copy-start.7
  0.7 0.1 copy.10.part
  0.8 0.6 %copy-done.6 = s32[2,3]{1,0:T(2,128)S(1)} copy-done((s32[2,3]{1,0:T(2,128)S(1)}, s32[2,3]{1,0:T(2,128)}, u32[]{:S(2)}) %copy-start.6) | copy-done | bytes 48
  1.4 0.0 copy-done.7
  1.4 0.0 copy-start
  1.4 0.9 %copy-done = bf16[256,512]{1,0:T(8,128)(2,1)S(1)} copy-done((bf16[256,512]{1,0:T(8,128)(2,1)S(1)}, bf16[256,512]{1,0:T(8,128)(2,1)}, u32[]{:S(2)}) %copy-start) | copy-done | bytes 262168
  2.3 0.0 copy-start.1
  2.3 0.9 %copy-done.1 = bf16[256,512]{1,0:T(8,128)(2,1)S(1)} copy-done((bf16[256,512]{1,0:T(8,128)(2,1)S(1)}, bf16[256,512]{1,0:T(8,128)(2,1)}, u32[]{:S(2)}) %copy-start.1) | copy-done | bytes 262168
  3.3 0.0 copy-start.2
  3.3 0.9 %copy-done.2 = bf16[512,256]{1,0:T(8,128)(2,1)S(1)} copy-done((bf16[512,256]{1,0:T(8,128)(2,1)S(1)}, bf16[512,256]{1,0:T(8,128)(2,1)}, u32[]{:S(2)}) %copy-start.2) | copy-done | bytes 262168
  4.2 0.0 copy-start.3
  4.2 0.9 %copy-done.3 = bf16[512,256]{1,0:T(8,128)(2,1)S(1)} copy-done((bf16[512,256]{1,0:T(8,128)(2,1)S(1)}, bf16[512,256]{1,0:T(8,128)(2,1)}, u32[]{:S(2)}) %copy-start.3) | copy-done | bytes 262168
  5.2 0.0 copy-start.4
  5.2 0.9 %copy-done.4 = bf16[512,256]{1,0:T(8,128)(2,1)S(1)} copy-done((bf16[512,256]{1,0:T(8,128)(2,1)S(1)}, bf16[512,256]{1,0:T(8,128)(2,1)}, u32[]{:S(2)}) %copy-start.4) | copy-done | bytes 262168
  6.1 0.0 copy-start.5
  6.1 0.9 %copy-done.5 = bf16[256,512]{1,0:T(8,128)(2,1)S(1)} copy-done((bf16[256,512]{1,0:T(8,128)(2,1)S(1)}, bf16[256,512]{1,0:T(8,128)(2,1)}, u32[]{:S(2)}) %copy-start.5) | copy-done | bytes 262168
  7.1 37.8 %shard_map.91 = bf16[256,256]{1,0:T(8,128)(2,1)S(1)} custom-call(bf16[256,512]{1,0:T(8,128)(2,1)S(1)} %copy-done, bf16[256,512]{1,0:T(8,128)(2,1)S(1)} %copy-done.1, bf16[512,256]{1,0:T(8,128)(2,1)S(1)} %copy-done.2, bf16[512,256]{1,0:T(8,128)(2,1)S(1)} %copy-done.3, bf16[512,256]{1,0:T(8,128)(2,1)S(1)} %copy-done.4, bf16[256,512]{1,0:T(8,128)(2,1)S(1)} %copy-done.5, ...), custom_call_target="tpu_custom_call" | custom-call | tf_op jit(solution)/shard_map/pallas_call | solution.py:343
  44.9 0.7 %copy.12 = bf16[256,256]{1,0:T(8,128)(2,1)} copy(bf16[256,256]{1,0:T(8,128)(2,1)S(1)} %shard_map.91) | data formatting | bytes 262144
Async XLA Ops:
  0.0 0.7 %copy-start.8 = (s32[3,2]{0,1:T(2,128)S(1)}, s32[3,2]{0,1:T(2,128)}, u32[]{:S(2)}) copy-start(s32[3,2]{0,1:T(2,128)} %param.16) | copy-start | bytes 76
  0.7 0.7 %copy-start.6 = (s32[2,3]{1,0:T(2,128)S(1)}, s32[2,3]{1,0:T(2,128)}, u32[]{:S(2)}) copy-start(s32[2,3]{1,0:T(2,128)} %adj.1) | copy-start | bytes 76
  0.7 0.7 %copy-start.7 = (s32[256]{0:T(256)S(1)}, s32[256]{0:T(256)}, u32[]{:S(2)}) copy-start(s32[256]{0:T(256)} %param.17) | copy-start | bytes 3076
  1.4 0.9 %copy-start = (bf16[256,512]{1,0:T(8,128)(2,1)S(1)}, bf16[256,512]{1,0:T(8,128)(2,1)}, u32[]{:S(2)}) copy-start(bf16[256,512]{1,0:T(8,128)(2,1)} %feat.1) | copy-start | bytes 786436
  2.3 0.9 %copy-start.1 = (bf16[256,512]{1,0:T(8,128)(2,1)S(1)}, bf16[256,512]{1,0:T(8,128)(2,1)}, u32[]{:S(2)}) copy-start(bf16[256,512]{1,0:T(8,128)(2,1)} %cot.1) | copy-start | bytes 786436
  3.3 0.9 %copy-start.2 = (bf16[512,256]{1,0:T(8,128)(2,1)S(1)}, bf16[512,256]{1,0:T(8,128)(2,1)}, u32[]{:S(2)}) copy-start(bf16[512,256]{1,0:T(8,128)(2,1)} %w_q.1) | copy-start | bytes 786436
  4.2 0.9 %copy-start.3 = (bf16[512,256]{1,0:T(8,128)(2,1)S(1)}, bf16[512,256]{1,0:T(8,128)(2,1)}, u32[]{:S(2)}) copy-start(bf16[512,256]{1,0:T(8,128)(2,1)} %w_k.1) | copy-start | bytes 786436
  5.2 0.9 %copy-start.4 = (bf16[512,256]{1,0:T(8,128)(2,1)S(1)}, bf16[512,256]{1,0:T(8,128)(2,1)}, u32[]{:S(2)}) copy-start(bf16[512,256]{1,0:T(8,128)(2,1)} %w_v.1) | copy-start | bytes 786436
  6.1 0.9 %copy-start.5 = (bf16[256,512]{1,0:T(8,128)(2,1)S(1)}, bf16[256,512]{1,0:T(8,128)(2,1)}, u32[]{:S(2)}) copy-start(bf16[256,512]{1,0:T(8,128)(2,1)} %w_o.1) | copy-start | bytes 786436

commit v2 on v1

--- a/solution.py
+++ b/solution.py
@@ -25,12 +25,13 @@
 
 def kernel(
     n, nb,
-    feat, cot, w_q, w_k, w_v, w_o, adj, part, order, out,
+    feat_hbm, cot_hbm, w_q_hbm, w_k_hbm, w_v_hbm, w_o_hbm, adj_hbm, part_hbm, order_hbm, out,
+    feat, cot, w_q, w_k, w_v, w_o, adj, part, order, fetch,
     perm, own_x, own_c, rx, rc, k_own, v_own, kt_own, qm_own, gm_own,
     kt_far, qm_far, s_loc, g_loc, s_far, g_far, s_back, peak, stat, stat_far,
     dq, dk, dv, give, take,
     x_send, x_recv, xf_send, xf_recv, c_send, c_recv, cf_send, cf_recv,
-    t_send, t_recv, h_send, h_recv,
+    t_send, t_recv, h_send, h_recv, hop_send,
 ):
     rows, width = feat.shape
     half = width // 2
@@ -45,13 +46,38 @@
     def onward(d):
         return {"slab": lax.rem(slab + d, n)}
 
+    line = n == 4
+    at_start, at_end = slab == 0, slab == n - 1
+    inner = jnp.logical_and(slab > 0, slab < n - 1)
+
     def each(f):
-        if n <= 4:
-            for d in sorted(range(1, n), key=lambda d: (min(d, n - d), d)):
+        if line:
+            f(jnp.where(at_start, 3, 1))
+            f(jnp.where(inner, 3, 2))
+            f(jnp.where(at_start, 1, jnp.where(at_end, 3, 2)))
+        elif n <= 4:
+            for d in range(1, n):
                 f(d)
         else:
             lax.fori_loop(1, n, lambda d, c: (f(d), c)[1], 0)
 
+    def each_direct(f):
+        if line:
+            f(2)
+            pl.when(jnp.logical_not(at_end))(lambda: f(1))
+            pl.when(jnp.logical_not(at_start))(lambda: f(3))
+        else:
+            each(f)
+
+    loads = [
+        pltpu.make_async_copy(src, dst, fetch.at[i])
+        for i, (src, dst) in enumerate((
+            (order_hbm, order), (feat_hbm, feat), (cot_hbm, cot), (w_q_hbm, w_q), (w_k_hbm, w_k),
+            (w_v_hbm, w_v), (w_o_hbm, w_o), (adj_hbm, adj), (part_hbm, part),
+        ))
+    ]
+    for load in loads:
+        load.start()
     barrier = pltpu.get_barrier_semaphore()
 
     def greet(where):
@@ -89,6 +115,32 @@
     x_twin = functools.partial(twin_copy, rx, xf_send, xf_recv)
     c_twin = functools.partial(twin_copy, rc, cf_send, cf_recv)
 
+    def hop_copy(far, recv, k):
+        up = slab == n - 2
+        slot = jnp.where(up, 3, 1)
+        return copy(
+            far.at[2, h], far.at[slot, h], hop_send.at[k], recv.at[slot],
+            {"slab": jnp.where(up, n - 1, 0)},
+        )
+
+    x_hop = functools.partial(hop_copy, rx, x_recv, 0)
+    c_hop = functools.partial(hop_copy, rc, c_recv, 1)
+
+    def pass_on(slab_copy_of, hop):
+        if line:
+            @pl.when(inner)
+            def _():
+                slab_copy_of(2).wait_recv()
+                hop().start()
+
+    def arrive(slab_copy_of, d):
+        if line:
+            pl.when(jnp.logical_not(jnp.logical_and(inner, d == 2)))(
+                lambda: slab_copy_of(d).wait_recv()
+            )
+        else:
+            slab_copy_of(d).wait_recv()
+
     def stat_near():
         return (
             copy(stat.at[0], stat_far.at[0, 1], t_send.at[n], t_recv.at[n], behind),
@@ -98,6 +150,8 @@
     def stat_slab(d):
         return copy(stat, stat_far.at[d], t_send.at[d], t_recv.at[d], onward(d))
 
+    loads[0].wait()
+    loads[1].wait()
     hot = lax.broadcasted_iota(jnp.int32, (rows, rows), 0) == order[...]
     perm[...] = jnp.where(hot, 1.0, 0.0).astype(BF16)
     x_all = lax.dot_general(perm[...], feat[...], TN, preferred_element_type=F32).astype(BF16)
@@ -106,8 +160,10 @@
     pl.semaphore_wait(barrier, n + 2)
     for c in x_near():
         c.start()
-    each(lambda d: x_slab(d).start())
-
+    each_direct(lambda d: x_slab(d).start())
+
+    for load in loads[2:]:
+        load.wait()
     c_all = lax.dot_general(perm[...], cot[...], TN, preferred_element_type=F32).astype(BF16)
     own_c[0] = c_all[:, :half]
     own_c[1] = c_all[:, half:]
@@ -128,7 +184,7 @@
         source = lax.rem(slab + n - i, n)
         total = jnp.float32(0.0)
         for m in range(3):
-            total = total + jnp.where(lax.div(part[m, b], 2 * nb) == source, 1.0, 0.0)
+            total = total + jnp.where(lax.div(part[b, m], 2 * nb) == source, 1.0, 0.0)
         return total
 
     def local_weight(kb, qb):
@@ -150,7 +206,7 @@
         gm_own[b] = masked(g_all, b)
     for c in c_near():
         c.start()
-    each(lambda d: c_slab(d).start())
+    each_direct(lambda d: c_slab(d).start())
     for b in range(2):
         s = mm_nt(k_own[...], qm_own[b])
         s_loc[b] = s
@@ -184,6 +240,7 @@
             top = jnp.max(s, axis=0, keepdims=True) + bias(far_weight(i, b))
             peak[b] = jnp.maximum(peak[b], top)
 
+    pass_on(x_slab, x_hop)
     for c in x_near():
         c.wait_recv()
     x_twin(0).start()
@@ -191,7 +248,7 @@
     forward_slot(0)
 
     def take_x(d):
-        x_slab(d).wait_recv()
+        arrive(x_slab, d)
         x_twin(d).start()
         x_twin(d).wait_recv()
         forward_slot(d)
@@ -289,6 +346,7 @@
             dv[here, :] += mm(p.astype(BF16), gm)
             dk[here, :] += mm(ds, qm_far[i, b])
 
+    pass_on(c_slab, c_hop)
     for c in c_near():
         c.wait_recv()
     c_twin(0).start()
@@ -298,7 +356,7 @@
     backward_slot(0)
 
     def take_c(d):
-        c_slab(d).wait_recv()
+        arrive(c_slab, d)
         c_twin(d).start()
         c_twin(d).wait_recv()
         stat_slab(d).wait_recv()
@@ -326,10 +384,17 @@
         c.wait_send()
 
     def finish(d):
-        for c in (x_slab(d), c_slab(d), stat_slab(d), x_twin(d), c_twin(d)):
+        for c in (stat_slab(d), x_twin(d), c_twin(d)):
             c.wait_send()
 
     each(finish)
+    each_direct(lambda d: x_slab(d).wait_send())
+    each_direct(lambda d: c_slab(d).wait_send())
+    if line:
+        @pl.when(inner)
+        def _():
+            x_hop().wait_send()
+            c_hop().wait_send()
 
 
 def body(features, cotangent, w_query, w_key, w_value, w_out, adjacency, partner, node_order):
@@ -339,13 +404,17 @@
     half, block = width // 2, rows // 2
     lanes = (cols // HEAD_DIM) * block
     vm, dma = pltpu.VMEM, pltpu.SemaphoreType.DMA
-    vmem, smem = (pl.BlockSpec(memory_space=m) for m in (pltpu.VMEM, pltpu.SMEM))
+    vmem, hbm = (pl.BlockSpec(memory_space=m) for m in (pltpu.VMEM, pltpu.HBM))
     return pl.pallas_call(
         functools.partial(kernel, n, nb),
         out_shape=jax.ShapeDtypeStruct((rows, half), BF16),
-        in_specs=[vmem] * 6 + [smem] * 2 + [vmem],
+        in_specs=[hbm] * 9,
         out_specs=vmem,
         scratch_shapes=[
+            vm((rows, width), BF16), vm((rows, width), BF16),
+            vm((width, cols), BF16), vm((width, cols), BF16), vm((width, cols), BF16),
+            vm((cols, width), BF16), pltpu.SMEM(adjacency.shape, jnp.int32),
+            pltpu.SMEM(adjacency.shape, jnp.int32), vm((1, rows), jnp.int32), dma((9,)),
             vm((rows, rows), BF16),
             vm((2, rows, half), BF16), vm((2, rows, half), BF16),
             vm((n, 2, rows, half), BF16), vm((n, 2, rows, half), BF16),
@@ -359,13 +428,13 @@
             vm((cols, rows), F32), vm((rows, cols), F32), vm((rows, cols), F32),
             vm((rows, half), BF16), vm((rows, half), BF16),
         ] + [dma((n + 1,)), dma((n + 1,)), dma((n,)), dma((n,))] * 2
-        + [dma((n + 1,)), dma((n + 1,)), dma(()), dma(())],
+        + [dma((n + 1,)), dma((n + 1,)), dma(()), dma(()), dma((2,))],
         compiler_params=pltpu.CompilerParams(
-            collective_id=0, has_side_effects=True, vmem_limit_bytes=52 * 1024 * 1024
+            collective_id=0, has_side_effects=True, vmem_limit_bytes=63 * 1024 * 1024
         ),
     )(
         features, cotangent, w_query, w_key, w_value, w_out,
-        adjacency, partner, node_order.reshape(1, rows),
+        adjacency, partner.T, node_order.reshape(1, rows),
     )
 
 

time: 45.9 us -> 37 us (0.81)
  the two profiles are of different devices: /device:TPU:0 before, /device:TPU:17 now
where the time goes in v2:
time: 37 us; the launch traced here: 36.8 us
  Pallas kernels  35.2 us (95%)
  local copies, waits for them, and re-layouts  1.57 us (4%)
    pallas_call x1, Pallas kernels, body(): pl.pallas_call(functools.partial(kernel, n, nb), out_shape=jax.ShapeDtype...  35.2 us
    unnamed x1, local copies, waits for them, and re-layouts  1.57 us

profile of v2, /device:TPU:17, one launch (start us, length us, event | category | flops | bytes accessed | tf_op | source)
XLA Modules:
  0.0 36.8 jit_solution(6603909202120335819)
XLA Ops:
  0.0 35.2 %shard_map.91 = bf16[256,256]{1,0:T(8,128)(2,1)} custom-call(bf16[256,512]{1,0:T(8,128)(2,1)} %feat_hbm.1, bf16[256,512]{1,0:T(8,128)(2,1)} %cot_hbm.1, bf16[512,256]{1,0:T(8,128)(2,1)} %w_q_hbm.1, bf16[512,256]{1,0:T(8,128)(2,1)} %w_k_hbm.1, bf16[512,256]{1,0:T(8,128)(2,1)} %w_v_hbm.1, bf16[256,512]{1,0:T(8,128)(2,1)} %w_o_hbm.1, s32[2,3]{1,0:T(2,128)} %adj_hbm.1, ...), custom_call_target="tpu_custom_call" | custom-call | tf_op jit(solution)/shard_map/pallas_call | solution.py:408
  35.3 1.6 %copy.11 = bf16[256,256]{1,0:T(8,128)(2,1)} copy(bf16[256,256]{1,0:T(8,128)(2,1)} %shard_map.91) | data formatting | bytes 262144

commit v3 on v2

--- a/solution.py
+++ b/solution.py
@@ -31,7 +31,7 @@
     kt_far, qm_far, s_loc, g_loc, s_far, g_far, s_back, peak, stat, stat_far,
     dq, dk, dv, give, take,
     x_send, x_recv, xf_send, xf_recv, c_send, c_recv, cf_send, cf_recv,
-    t_send, t_recv, h_send, h_recv, hop_send,
+    t_send, t_recv, h_send, h_recv, hop_send, part_out,
 ):
     rows, width = feat.shape
     half = width // 2
@@ -61,6 +61,30 @@
         else:
             lax.fori_loop(1, n, lambda d, c: (f(d), c)[1], 0)
 
+    def stream(arrived, twin_of, work):
+        if line:
+            order_of = [
+                0, jnp.where(at_start, 3, 1), jnp.where(inner, 3, 2),
+                jnp.where(at_start, 1, jnp.where(at_end, 3, 2)),
+            ]
+            arrived(0)
+            twin_of(0).start()
+            for at, now in enumerate(order_of):
+                if at + 1 < n:
+                    arrived(order_of[at + 1])
+                    twin_of(order_of[at + 1]).start()
+                twin_of(now).wait_recv()
+                work(now)
+        else:
+            def step(d):
+                arrived(d)
+                twin_of(d).start()
+                twin_of(d).wait_recv()
+                work(d)
+
+            step(0)
+            each(step)
+
     def each_direct(f):
         if line:
             f(2)
@@ -157,10 +181,6 @@
     x_all = lax.dot_general(perm[...], feat[...], TN, preferred_element_type=F32).astype(BF16)
     own_x[0] = x_all[:, :half]
     own_x[1] = x_all[:, half:]
-    pl.semaphore_wait(barrier, n + 2)
-    for c in x_near():
-        c.start()
-    each_direct(lambda d: x_slab(d).start())
 
     for load in loads[2:]:
         load.wait()
@@ -204,9 +224,10 @@
     for b in range(2):
         qm_own[b] = masked(q_all, b)
         gm_own[b] = masked(g_all, b)
-    for c in c_near():
+    pl.semaphore_wait(barrier, n + 2)
+    for c in x_near():
         c.start()
-    each_direct(lambda d: c_slab(d).start())
+    each_direct(lambda d: x_slab(d).start())
     for b in range(2):
         s = mm_nt(k_own[...], qm_own[b])
         s_loc[b] = s
@@ -241,19 +262,21 @@
             peak[b] = jnp.maximum(peak[b], top)
 
     pass_on(x_slab, x_hop)
-    for c in x_near():
-        c.wait_recv()
-    x_twin(0).start()
-    x_twin(0).wait_recv()
-    forward_slot(0)
-
-    def take_x(d):
-        arrive(x_slab, d)
-        x_twin(d).start()
-        x_twin(d).wait_recv()
-        forward_slot(d)
-
-    each(take_x)
+    def x_arrived(d):
+        if isinstance(d, int) and d == 0:
+            for c in x_near():
+                c.wait_recv()
+        else:
+            arrive(x_slab, d)
+
+    def forward_step(i):
+        forward_slot(i)
+        if isinstance(i, int) and i == 0:
+            for c in c_near():
+                c.start()
+            each_direct(lambda d: c_slab(d).start())
+
+    stream(x_arrived, x_twin, forward_step)
 
     for b in range(2):
         qcols = slice(b * block, (b + 1) * block)
@@ -347,34 +370,33 @@
             dk[here, :] += mm(ds, qm_far[i, b])
 
     pass_on(c_slab, c_hop)
-    for c in c_near():
-        c.wait_recv()
-    c_twin(0).start()
-    c_twin(0).wait_recv()
-    for c in stat_near():
-        c.wait_recv()
-    backward_slot(0)
-
-    def take_c(d):
-        arrive(c_slab, d)
-        c_twin(d).start()
-        c_twin(d).wait_recv()
-        stat_slab(d).wait_recv()
-        backward_slot(d)
-
-    each(take_c)
+    def c_arrived(d):
+        if isinstance(d, int) and d == 0:
+            for c in (*c_near(), *stat_near()):
+                c.wait_recv()
+        else:
+            arrive(c_slab, d)
+            stat_slab(d).wait_recv()
 
     dq_low = (dq[...].T * scale).astype(BF16)
+
+    def half_at(which):
+        return pl.ds(pl.multiple_of(which * half, half), half)
+
+    for k, which in enumerate((1 - h, h)):
+        part_out[k] = mm_nt(dq_low, w_q[half_at(which), :])
+    stream(c_arrived, c_twin, backward_slot)
+
     dk_low, dv_low = dk[...].astype(BF16), dv[...].astype(BF16)
 
-    def share(which):
-        at = pl.ds(pl.multiple_of(which * half, half), half)
-        return mm_nt(dq_low, w_q[at, :]) + mm_nt(dk_low, w_k[at, :]) + mm_nt(dv_low, w_v[at, :])
-
-    give[...] = share(1 - h).astype(BF16)
+    def share(k, which):
+        at = half_at(which)
+        return part_out[k] + mm_nt(dk_low, w_k[at, :]) + mm_nt(dv_low, w_v[at, :])
+
+    give[...] = share(0, 1 - h).astype(BF16)
     swap = copy(give, take, h_send, h_recv, twin)
     swap.start()
-    mine = share(h)
+    mine = share(1, h)
     swap.wait_recv()
     branch = (mine + take[...].astype(F32)).astype(BF16)
     out[...] = mm(perm[...], branch).astype(BF16)
@@ -428,7 +450,7 @@
             vm((cols, rows), F32), vm((rows, cols), F32), vm((rows, cols), F32),
             vm((rows, half), BF16), vm((rows, half), BF16),
         ] + [dma((n + 1,)), dma((n + 1,)), dma((n,)), dma((n,))] * 2
-        + [dma((n + 1,)), dma((n + 1,)), dma(()), dma(()), dma((2,))],
+        + [dma((n + 1,)), dma((n + 1,)), dma(()), dma(()), dma((2,)), vm((2, rows, half), F32)],
         compiler_params=pltpu.CompilerParams(
             collective_id=0, has_side_effects=True, vmem_limit_bytes=63 * 1024 * 1024
         ),

time: 37 us -> 34.1 us (0.922)
  the two profiles are of different devices: /device:TPU:17 before, /device:TPU:0 now
where the time goes in v3:
time: 34.1 us; the launch traced here: 34 us
  Pallas kernels  32.4 us (95%)
  local copies, waits for them, and re-layouts  1.57 us (5%)
    pallas_call x1, Pallas kernels, body(): pl.pallas_call(functools.partial(kernel, n, nb), out_shape=jax.ShapeDtype...  32.4 us
    unnamed x1, local copies, waits for them, and re-layouts  1.57 us

profile of v3, /device:TPU:0, one launch (start us, length us, event | category | flops | bytes accessed | tf_op | source)
XLA Modules:
  0.0 34.0 jit_solution(643919928322171398)
XLA Ops:
  0.0 32.4 %shard_map.91 = bf16[256,256]{1,0:T(8,128)(2,1)} custom-call(bf16[256,512]{1,0:T(8,128)(2,1)} %feat_hbm.1, bf16[256,512]{1,0:T(8,128)(2,1)} %cot_hbm.1, bf16[512,256]{1,0:T(8,128)(2,1)} %w_q_hbm.1, bf16[512,256]{1,0:T(8,128)(2,1)} %w_k_hbm.1, bf16[512,256]{1,0:T(8,128)(2,1)} %w_v_hbm.1, bf16[256,512]{1,0:T(8,128)(2,1)} %w_o_hbm.1, s32[2,3]{1,0:T(2,128)} %adj_hbm.1, ...), custom_call_target="tpu_custom_call" | custom-call | tf_op jit(solution)/shard_map/pallas_call | solution.py:430
  32.4 1.6 %copy.11 = bf16[256,256]{1,0:T(8,128)(2,1)} copy(bf16[256,256]{1,0:T(8,128)(2,1)} %shard_map.91) | data formatting | bytes 262144
